TPU v7x, 256 devices: a whole 4x4x8 slice. The times are simulated.
256 devices in a mesh: pair: 4 (over y_hi, core), cd: 64 (over z, x, y_lo).
Axes of the slice: x: 4, y: 4 (y_hi: 2, y_lo: 2; y = y_hi * 2 + y_lo), z: 8, core: 2. Of those that a mesh axis runs over, the one named last changes fastest.
Arguments:
- lambda_amps: bfloat16 [11264, 1024], P('pair'), may hold values from -0.0546875 to 0.0546875
- t_amps: bfloat16 [11264, 1024], P('pair', 'cd'), may hold values from -6 to 6
- coef_mu: float32 [768, 64], P('pair'), may hold values from -0.75 to 0.75
- coef_nu: float32 [768, 16], replicated, may hold values from -1.5 to 1.5
Outputs:
- half_ao: bfloat16 [768, 768, 1024], P('pair', 'cd')
All inputs are finite; a program needn't handle non-finite values.
Results may differ from a plain program's by a relative error of at most 0.001.
Values sent between devices are 32-bit elements; how exact they have to be, the bound alone decides.
A program may use at most 64 MiB of HBM per device.

v0:
```python
import jax
import jax.numpy as jnp
from jax import lax
from jax.sharding import PartitionSpec as P

A = 64
B = 16


def cut_along(array, dim, peers):
    before, after = (array.shape[:dim], array.shape[dim + 1 :])
    return jnp.moveaxis(array.reshape(*before, peers, -1, *after), dim, 0)


def sent_and_summed(array, axis, dim):
    blocks = cut_along(array, dim, lax.axis_size(axis))
    arrived = lax.all_to_all(blocks, axis, split_axis=0, concat_axis=0, tiled=True)
    return arrived.sum(axis=0)


def body(lambda_amps, t_amps, coef_mu, coef_nu):
    partial_value = lax.dot_general(
        lambda_amps, t_amps, (((0,), (0,)), ((), ())), preferred_element_type=jnp.float32
    )
    local_cols = partial_value.shape[1]
    groups = lax.axis_size("pair")
    share = sent_and_summed(partial_value.reshape(A, B * local_cols), "pair", 0)
    panel = share.reshape(A // groups, B, local_cols)
    half = jnp.einsum("abc,nb->nac", panel, coef_nu, precision=lax.Precision.HIGHEST)
    moved = lax.all_to_all(half, "cd", split_axis=0, concat_axis=2, tiled=True)
    gathered = lax.all_gather(moved, "pair", axis=1, tiled=True)
    result = jnp.einsum("ma,nac->mnc", coef_mu, gathered, precision=lax.Precision.HIGHEST)
    return result.astype(jnp.bfloat16)


def solution(mesh):
    in_specs = (P("pair", None), P("pair", "cd"), P("pair", None), P())
    out_specs = P("pair", "cd", None)
    return jax.shard_map(body, mesh=mesh, in_specs=in_specs, out_specs=out_specs, check_vma=False)
```

profile of v0, /device:TPU:1, one launch (start us, length us, event | category | flops | bytes accessed | tf_op | source)
XLA Modules:
  0.0 139.2 jit_solution(14465179184034495695)
XLA Ops:
  6.5 0.0 copy-start
  6.5 0.0 copy-start.2
  6.5 0.0 all-gather.2.cloned.1.call-start
  6.5 0.9 copy-done
  7.4 4.3 %fusion.2 = f32[1024,16]{1,0:T(8,128)S(1)} fusion(bf16[2816,1024]{1,0:T(8,128)(2,1)} %param.4, bf16[2816,16]{0,1:T(8,128)(2,1)S(1)} %copy-done), kind=kOutput, calls=%fused_computation.4 | convolution fusion | flops 92274688 | bytes 5922816 | tf_op jit(solution)/shard_map/dot_general | solution.py:22
  11.8 0.2 reshape_reshape.3
  12.0 10.5 %all_to_all.23 = f32[4,16,256]{2,1,0:T(8,128)S(1)} all-to-all(f32[4,16,256]{2,1,0:T(8,128)S(1)} %reshape_reshape.3), channel_id=1, replica_groups=mesh['pair'=4,'cd'=64] {'pair'}, dimensions={0} | all-to-all | bytes 131072 | tf_op jit(solution)/shard_map/all_to_all | solution.py:17
  22.5 0.1 reshape.3
  22.6 0.0 copy-done.2
  22.6 0.8 convolution_bitcast_fusion
  23.5 5.0 %copy.11 = f32[768,16,16]{2,1,0:T(8,128)} copy(f32[768,16,16]{0,2,1:T(8,128)S(1)} %convolution_bitcast_fusion) | data formatting | bytes 1572864 | tf_op jit(solution)/shard_map/abc,nb->nac/dot_general | solution.py:29
  28.5 4.8 %reshape.6 = f32[64,1,3072]{2,1,0:T(1,128)S(1)} reshape(f32[768,16,16]{2,1,0:T(8,128)} %copy.11) | data formatting | bytes 1572864
  33.2 32.1 %all_to_all.24 = f32[64,1,3072]{2,1,0:T(1,128)S(1)} all-to-all(f32[64,1,3072]{2,1,0:T(1,128)S(1)} %reshape.6), channel_id=1, replica_groups=mesh['pair'=4,'cd'=64] {'cd'}, dimensions={0} | all-to-all | bytes 1572864 | tf_op jit(solution)/shard_map/all_to_all | solution.py:30
  65.3 0.5 broadcast
  65.8 2.6 %reduce = f32[64,3072]{1,0:T(8,128)S(1)} reduce(f32[64,1,3072]{2,1,0:T(1,128)S(1)} %all_to_all.24, f32[]{:T(128)} %broadcast), dimensions={1}, to_apply=%all_to_all.17.reduce_sub_computation | reduce | bytes 1572868 | tf_op jit(solution)/shard_map/all_to_all | solution.py:30
  68.5 3.8 %reshape.7 = f32[768,16,16]{2,1,0:T(8,128)} reshape(f32[64,3072]{1,0:T(8,128)S(1)} %reduce) | data formatting | bytes 1572864
  72.3 9.1 %copy.13 = f32[12,16,64,16]{3,2,1,0:T(8,128)} copy(f32[12,16,64,16]{3,1,0,2:T(8,128)} %bitcast.20) | data formatting | bytes 1572864 | tf_op jit(solution)/shard_map/all_to_all | solution.py:30
  81.4 0.0 copy-start.1
  81.4 7.1 %all_to_all.20 = f32[12,16,1024]{2,1,0:T(8,128)} reshape(f32[12,16,64,16]{3,2,1,0:T(8,128)} %copy.13) | data formatting | bytes 1572864 | tf_op jit(solution)/shard_map/all_to_all | solution.py:30
  88.5 0.0 all-gather.2.cloned.1.call-update
  88.5 33.2 %all-gather.2.cloned.1.call-done = f32[12,64,1024]{2,1,0:T(8,128)} async-done(((f32[12,16,1024]{2,1,0:T(8,128)}), f32[12,64,1024]{2,1,0:T(8,128)}) %all-gather.2.cloned.1.call-update) | async-done | bytes 3145744 | tf_op jit(solution)/shard_map/all_gather | solution.py:31
  121.7 0.0 copy-done.1
  121.7 10.6 %convert_bitcast_fusion = bf16[192,12,1024]{2,0,1:T(8,128)(2,1)} fusion(f32[12,64,1024]{2,1,0:T(8,128)} %all-gather.2.cloned.1.call-done, f32[192,64]{0,1:T(8,128)S(1)} %copy-done.1), kind=kOutput, calls=%fused_computation | convolution fusion | flops 1814298624 | bytes 7913472 | tf_op jit(solution)/shard_map/ma,nac->mnc/dot_general | solution.py:32
  (1 shorter events, 0.0 us)
Async XLA Ops:
  6.5 0.9 copy-start
  6.5 16.1 %copy-start.2 = (f32[768,16]{0,1:T(8,128)S(1)}, f32[768,16]{0,1:T(8,128)}, u32[]{:S(2)}) copy-start(f32[768,16]{0,1:T(8,128)} %param.7) | copy-start | bytes 147460
  6.5 115.2 %all-gather.2.cloned.1.call-start = ((), (), s32[]{:S(2)}) async-start(), calls=%async_computation.2 | async-start | bytes 3932160 | tf_op jit(solution)/shard_map/all_gather | solution.py:31
  81.4 40.3 %copy-start.1 = (f32[192,64]{0,1:T(8,128)S(1)}, f32[192,64]{0,1:T(8,128)}, u32[]{:S(2)}) copy-start(f32[192,64]{0,1:T(8,128)} %param.6) | copy-start | bytes 147460
Sparse Core Ops, SparseCore 0:
  88.7 33.0 all-gather.1
where the time goes:
time: 140 us; the launch traced here: 139 us
  blocking collectives  42.6 us (30%)
  waiting for transfers between devices  33.2 us (24%)
  local copies, waits for them, and re-layouts  31.5 us (22%)
  matrix products  15.8 us (11%)
  between operations  13.4 us (10%)
  other arithmetic  2.61 us (2%)
    all_gather x1, waiting for transfers between devices, body(): gathered = lax.all_gather(moved, 'pair', axis=1, tiled=True)  33.2 us
    all_to_all x1, blocking collectives, body(): moved = lax.all_to_all(half, 'cd', split_axis=0, concat_axis=2, tiled=True)  32.1 us
    all_to_all x3, local copies, waits for them, and re-layouts, body(): moved = lax.all_to_all(half, 'cd', split_axis=0, concat_axis=2, tiled=True)  16.7 us
    dot_general x1, matrix products, body(): jnp.einsum('ma,nac->mnc', coef_mu, gathered, precision=lax.Precision.HIGH...  10.6 us
    all_to_all x1, blocking collectives, sent_and_summed(): lax.all_to_all(blocks, axis, split_axis=0, concat_axis=0, tiled=True)  10.5 us
    unnamed x8, local copies, waits for them, and re-layouts  9.51 us
    dot_general x1, local copies, waits for them, and re-layouts, body(): jnp.einsum('abc,nb->nac', panel, coef_nu, precision=lax.Precision.HIGHEST)  4.98 us
    dot_general x1, matrix products, body(): lax.dot_general(lambda_amps, t_amps, (((0,), (0,)), ((), ())), preferred_...  4.33 us
  transfers between devices with their start and end apart: 1, of which 1 were waited for; matrix products, arithmetic and copies ran while one was open for 0% of the time, Pallas kernels for 0%

commit v1 on v0

v1 whole, which is shorter than its diff:
```python
import jax
import jax.numpy as jnp
from jax import lax
from jax.experimental import pallas as pl
from jax.experimental.pallas import tpu as pltpu
from jax.sharding import PartitionSpec as P

A = 64
B = 16
NX, NY, NZ = 4, 4, 8
MESH = pl.DeviceIdType.MESH
F32, BF16 = jnp.float32, jnp.bfloat16


class Place:
    def __init__(self):
        pair, cd = lax.axis_index("pair"), lax.axis_index("cd")
        self.core = pair % 2
        self.z = cd // 8
        self.x = (cd // 2) % 4
        self.y = (pair // 2) * 2 + cd % 2
        self.u = self.x + self.core * (self.y - self.x)
        self.v = self.y + self.core * (self.x - self.y)

    def seat(self, core, x, y, z):
        return ((y // 2) * 2 + core, z * 8 + x * 2 + y % 2)

    def far(self, other_core):
        core = (self.core + other_core) % 2
        return self.seat(core, self.x, (self.y + 2) % 4, self.z)

    def partner(self):
        return self.seat(1 - self.core, self.x, self.y, self.z)

    def ring(self, du=0, dv=0, dz=0):
        u, v, z = (self.u + du) % 4, (self.v + dv) % 4, (self.z + dz) % 8
        return self.seat(self.core, u + self.core * (v - u), v + self.core * (u - v), z)


def split(value):
    high = value.astype(BF16)
    return high, (value - high.astype(F32)).astype(BF16)


def gather_kernel(lam_hbm, t_hbm, mu_ref, nu_ref, g_ref, w_ref, m_ref,
                  lam, t_vmem, part, came, lam_sem, t_sem,
                  rs_send, rs_recv, u_send, u_recv, z_send, z_recv, v_send, v_recv, x_send, x_recv):
    me = Place()
    rows = lam_hbm.shape[0]
    pair = lax.axis_index("pair")
    far_same = (pair + 2) % 4
    far_other = ((pair // 2 + 1) % 2) * 2 + 1 - me.core
    near = (pair // 2) * 2 + 1 - me.core
    quarters = [far_same, far_other, near, pair]

    t_copy = pltpu.make_async_copy(t_hbm, t_vmem, t_sem)
    t_copy.start()
    lam_copies = []
    for i, q in enumerate(quarters):
        cols = pl.ds(pl.multiple_of(q * 256, 256), 256)
        copy = pltpu.make_async_copy(lam_hbm.at[:, cols], lam.at[i], lam_sem.at[i])
        copy.start()
        lam_copies.append(copy)

    greeted = [me.far(0), me.far(1), me.partner(), me.ring(du=1), me.ring(du=-1), me.ring(du=2),
               me.ring(dz=1), me.ring(dz=-1), me.ring(dz=2), me.ring(dz=-2), me.ring(dv=1), me.ring(dv=-1)]
    barrier = pltpu.get_barrier_semaphore()
    for peer in greeted:
        pl.semaphore_signal(barrier, inc=1, device_id=peer, device_id_type=MESH)

    sends = []

    def send(src, dst, ssem, rsem, peer):
        copy = pltpu.make_async_remote_copy(src, dst, ssem, rsem, device_id=peer, device_id_type=MESH)
        copy.start()
        sends.append(copy)

    def arrived(dst, ssem, rsem):
        pltpu.make_async_remote_copy(dst, dst, ssem, rsem, device_id=me.partner(), device_id_type=MESH).wait_recv()

    t_copy.wait()
    t_value = t_vmem[...]
    for i in range(4):
        lam_copies[i].wait()
        part[i] = jnp.dot(t_value, lam[i], preferred_element_type=F32)
        if i == 0:
            pl.semaphore_wait(barrier, len(greeted))
        if i < 3:
            peer = (me.far(0), me.far(1), me.partner())[i]
            send(part.at[i], came.at[i], rs_send.at[i], rs_recv.at[i], peer)

    first = lax.axis_index("cd") * 12
    pick = (lax.broadcasted_iota(jnp.int32, (192, 768), 1)
            == first + lax.broadcasted_iota(jnp.int32, (192, 768), 0) // 16).astype(F32).astype(BF16)
    spread = (lax.broadcasted_iota(jnp.int32, (16, 256), 1) % 16
              == lax.broadcasted_iota(jnp.int32, (16, 256), 0)).astype(F32).astype(BF16)
    own_a = (lax.broadcasted_iota(jnp.int32, (192, 256), 1) // 16
             == lax.broadcasted_iota(jnp.int32, (192, 256), 0) % 16)
    for i, term in enumerate(split(nu_ref[...])):
        taken = lax.dot_general(pick, term, (((1,), (1,)), ((), ())), preferred_element_type=F32)
        tiled = jnp.dot(taken.astype(BF16), spread, preferred_element_type=F32)
        w_ref[i] = jnp.where(own_a, tiled, 0.0).astype(BF16)
    mu_value = mu_ref[...]
    mu_high = mu_value.astype(BF16).astype(F32)
    m_ref[...] = jnp.concatenate([mu_high, mu_high, mu_value - mu_high], axis=0).T.astype(BF16)

    for i in range(3):
        arrived(came.at[i], rs_send.at[i], rs_recv.at[i])
    mine = g_ref.at[me.core]
    mine[me.v, me.z, me.u] = (part[3] + came[2]) + (came[0] + came[1])

    u_of = [(me.u + d) % 4 for d in range(4)]
    v_of = [(me.v + d) % 4 for d in range(4)]
    z_of = [(me.z + d) % 8 for d in range(8)]

    def block(dv, dz, du):
        return mine.at[v_of[dv % 4], z_of[dz % 8], u_of[du % 4]]

    def send_u(delta):
        slot = (delta % 4) - 1
        send(block(0, 0, 0), block(0, 0, 0), u_send.at[slot], u_recv.at[slot], me.ring(du=delta))

    def got_u(du):
        slot = (-du % 4) - 1
        arrived(block(0, 0, du), u_send.at[slot], u_recv.at[slot])

    def send_z(du, dz, delta):
        slot = (dz - delta) % 8 - 1
        send(block(0, dz, du), block(0, dz, du), z_send.at[du, slot], z_recv.at[du, slot], me.ring(dz=delta))

    def got_z(du, dz):
        slot = dz % 8 - 1
        arrived(block(0, dz, du), z_send.at[du, slot], z_recv.at[du, slot])

    def unit(dv, dz):
        return mine.at[v_of[dv % 4], z_of[dz % 8]]

    def half(dv, dz, h):
        return mine.at[v_of[dv % 4], z_of[dz % 8], pl.ds(2 * h, 2)]

    def send_v(dz):
        for i, delta in enumerate((1, -1)):
            send(unit(0, dz), unit(0, dz), v_send.at[dz % 8, i], v_recv.at[dz % 8, i], me.ring(dv=delta))

    def got_v(dz, i):
        dv = (-1, 1)[i]
        arrived(unit(dv, dz), v_send.at[dz % 8, i], v_recv.at[dz % 8, i])
        send(half(dv, dz, i), half(dv, dz, i), v_send.at[dz % 8, 2 + i], v_recv.at[dz % 8, 2 + i],
             me.ring(dv=(1, -1)[i]))

    def got_v2(dz):
        for i in range(2):
            arrived(half(2, dz, i), v_send.at[dz % 8, 2 + i], v_recv.at[dz % 8, 2 + i])

    def share(dv, dz):
        send(unit(dv, dz), unit(dv, dz), x_send.at[dv % 4, dz % 8], x_recv.at[dv % 4, dz % 8], me.partner())

    def z_from_origin(du):
        for delta in (2, -2, 1, -1):
            send_z(du, 0, delta)

    def z_take(du, dz):
        got_z(du, dz)
        if dz == -2:
            if du < 2:
                send_z(du, -2, 2)
            send_z(du, -2, 1)
        if dz == 2:
            if du >= 2:
                send_z(du, 2, -2)
            send_z(du, 2, -1)

    def unit_ready(dz):
        send_v(dz)
        share(0, dz)

    def v_take(dz):
        for i in range(2):
            got_v(dz, i)
            share((-1, 1)[i], dz)

    def v2_take(dz):
        got_v2(dz)
        share(2, dz)

    for delta in (2, 1, -1):
        send_u(delta)
    z_from_origin(0)
    for du in (1, 3, 2):
        got_u(du)
        z_from_origin(du)
    unit_ready(0)
    for du in (0, 1, 3, 2):
        for dz in (-2, 2):
            z_take(du, dz)
        for dz in (-1, 1):
            z_take(du, dz)
    for dz in (-2, 2, 1, -1):
        unit_ready(dz)
    v_take(0)
    for du in (0, 1, 3, 2):
        for dz in (-3, 3, 4):
            z_take(du, dz)
    for dz in (4, -3, 3):
        unit_ready(dz)
    for dz in (-2, 2, 1, -1):
        v_take(dz)
    v2_take(0)
    for dz in (4, -3, 3):
        v_take(dz)
    for dz in (-2, 2, 1, -1, 4, -3, 3):
        v2_take(dz)
    theirs = g_ref.at[1 - me.core]
    for dv in range(4):
        for dz in range(8):
            arrived(theirs.at[dv, dz], x_send.at[dv, dz], x_recv.at[dv, dz])
    for copy in sends:
        copy.wait_send()


def transform_kernel(g_ref, w_ref, m_ref, out_ref):
    nt = (((1,), (1,)), ((), ()))
    w_high, w_low = w_ref[0], w_ref[1]
    halves = []
    for p in range(4):
        yh, core = p // 2, p % 2
        pieces = []
        for z in range(g_ref.shape[2]):
            for x in range(NX):
                for yl in range(2):
                    y = 2 * yh + yl
                    pieces.append(g_ref[0, y, z, x] if core == 0 else g_ref[1, x, z, y])
        high, low = split(jnp.concatenate(pieces, axis=0))
        value = lax.dot_general(w_high, high, nt, preferred_element_type=F32)
        value += lax.dot_general(w_high, low, nt, preferred_element_type=F32)
        value += lax.dot_general(w_low, high, nt, preferred_element_type=F32)
        halves.append(value)
    m = m_ref[...]
    for nu in range(12):
        rows = slice(nu * 16, nu * 16 + 16)
        high, low = split(jnp.concatenate([value[rows] for value in halves], axis=0))
        stacked = jnp.concatenate([high, low, high], axis=0)
        out_ref[nu] = jnp.dot(m, stacked, preferred_element_type=F32).astype(BF16)


def body(lambda_amps, t_amps, coef_mu, coef_nu):
    rows = lambda_amps.shape[0]
    any_space = pl.BlockSpec(memory_space=pl.ANY)
    vmem = pl.BlockSpec(memory_space=pltpu.VMEM)
    dma = pltpu.SemaphoreType.DMA
    g, w, m = pl.pallas_call(
        gather_kernel,
        out_shape=(
            jax.ShapeDtypeStruct((2, 4, NZ, 4, 16, 256), F32),
            jax.ShapeDtypeStruct((2, 192, 256), BF16),
            jax.ShapeDtypeStruct((192, 192), BF16),
        ),
        in_specs=[any_space, any_space, vmem, vmem],
        out_specs=(vmem, vmem, vmem),
        scratch_shapes=[
            pltpu.VMEM((4, rows, 256), BF16),
            pltpu.VMEM((16, rows), BF16),
            pltpu.VMEM((4, 16, 256), F32),
            pltpu.VMEM((3, 16, 256), F32),
            dma((4,)), dma,
            dma((3,)), dma((3,)),
            dma((3,)), dma((3,)),
            dma((4, 7)), dma((4, 7)),
            dma((8, 4)), dma((8, 4)),
            dma((4, 8)), dma((4, 8)),
        ],
        compiler_params=pltpu.CompilerParams(collective_id=0, has_side_effects=True),
        name="gather",
    )(lambda_amps, t_amps.T, coef_mu.T, coef_nu.T)
    zt = 2
    out = pl.pallas_call(
        transform_kernel,
        grid=(NZ // zt,),
        out_shape=jax.ShapeDtypeStruct((12, 192, 1024), BF16),
        in_specs=[
            pl.BlockSpec((2, 4, zt, 4, 16, 256), lambda i: (0, 0, i, 0, 0, 0)),
            pl.BlockSpec((2, 192, 256), lambda i: (0, 0, 0)),
            pl.BlockSpec((192, 192), lambda i: (0, 0)),
        ],
        out_specs=pl.BlockSpec((12, 192, zt * 128), lambda i: (0, 0, i)),
        name="transform",
    )(g, w, m)
    return jnp.transpose(out, (1, 0, 2))


def solution(mesh):
    in_specs = (P("pair", None), P("pair", "cd"), P("pair", None), P())
    out_specs = P("pair", "cd", None)
    return jax.shard_map(body, mesh=mesh, in_specs=in_specs, out_specs=out_specs, check_vma=False)
```

time: 140 us -> 47.7 us (0.34)
  Pallas kernels: 0 us -> 47.4 us
  blocking collectives: 42.6 us -> 0 us
  waiting for transfers between devices: 33.2 us -> 0 us
  local copies, waits for them, and re-layouts: 31.5 us -> 0 us
  matrix products: 15.8 us -> 0 us
  between operations: 13.4 us -> 0.01 us
  other arithmetic: 2.61 us -> 0 us
    pallas_call x0 -> x2, Pallas kernels: none -> 47.4 us  [the longest x1 40.1 us: body(): pl.pallas_call(gather_kernel, out_shape=(jax.ShapeDtypeStruct((2, 4, NZ,...]
    all_to_all x2 -> x0, blocking collectives: 42.6 us -> none  [the longest x1 32.1 us: body(): moved = lax.all_to_all(half, 'cd', split_axis=0, concat_axis=2, tiled=True)]
    all_gather x1 -> x0, waiting for transfers between devices: 33.2 us -> none  [body(): gathered = lax.all_gather(moved, 'pair', axis=1, tiled=True)]
    all_to_all x3 -> x0, local copies, waits for them, and re-layouts: 16.7 us -> none  [body(): moved = lax.all_to_all(half, 'cd', split_axis=0, concat_axis=2, tiled=True)]
    dot_general x3 -> x0, matrix products: 15.8 us -> none  [the longest x1 10.6 us: body(): jnp.einsum('ma,nac->mnc', coef_mu, gathered, precision=lax.Precision.HIGH...]
    unnamed x8 -> x0, local copies, waits for them, and re-layouts: 9.51 us -> none
    dot_general x1 -> x0, local copies, waits for them, and re-layouts: 4.98 us -> none  [body(): jnp.einsum('abc,nb->nac', panel, coef_nu, precision=lax.Precision.HIGHEST)]
    all_to_all x1 -> x0, other arithmetic: 2.6 us -> none  [body(): moved = lax.all_to_all(half, 'cd', split_axis=0, concat_axis=2, tiled=True)]
  transfers between devices with their start and end apart: 1 -> 0, of which waited for: 1 -> 0; matrix products, arithmetic and copies ran while one was open for 0% -> 0% of each run, Pallas kernels for 0% -> 0%
where the time goes in v1:
time: 47.7 us; the launch traced here: 47.4 us
  Pallas kernels  47.4 us (99%)
    pallas_call x1, Pallas kernels, body(): pl.pallas_call(gather_kernel, out_shape=(jax.ShapeDtypeStruct((2, 4, NZ,...  40.1 us
    pallas_call x1, Pallas kernels, body(): pl.pallas_call(transform_kernel, grid=(NZ // zt,), out_shape=jax.ShapeDty...  7.34 us

profile of v1, /device:TPU:1, one launch (start us, length us, event | category | flops | bytes accessed | tf_op | source)
XLA Modules:
  0.0 47.4 jit_solution(10052551945892518229)
XLA Ops:
  0.0 40.1 %gather.1 = (f32[2,4,8,4,16,256]{5,4,3,2,1,0:T(8,128)}, bf16[2,192,256]{2,1,0:T(8,128)(2,1)}, bf16[192,192]{1,0:T(8,128)(2,1)}) custom-call(bf16[2816,1024]{1,0:T(8,128)(2,1)} %lam_hbm.1, bf16[16,2816]{1,0:T(8,128)(2,1)} %bitcast.4, f32[64,192]{1,0:T(8,128)} %bitcast.5, f32[16,768]{1,0:T(8,128)} %bitcast.6), custom_call_target="tpu_custom_call" | custom-call | tf_op jit(solution)/shard_map/gather/pallas_call | solution.py:251
  40.1 7.3 %transform.1 = bf16[12,192,1024]{2,1,0:T(8,128)(2,1)} custom-call(f32[2,4,8,4,16,256]{5,4,3,2,1,0:T(8,128)} %get-tuple-element.8.g_ref, bf16[2,192,256]{2,1,0:T(8,128)(2,1)} %get-tuple-element.9.w_ref, bf16[192,192]{1,0:T(8,128)(2,1)} %get-tuple-element.10.m_ref), custom_call_target="tpu_custom_call" | custom-call | tf_op jit(solution)/shard_map/transform/pallas_call | solution.py:276

commit v2 on v0

v2 whole, which is shorter than its diff:
```python
import jax
import jax.numpy as jnp
from jax import lax
from jax.experimental import pallas as pl
from jax.experimental.pallas import tpu as pltpu
from jax.sharding import PartitionSpec as P

A = 64
B = 16
NX, NY, NZ = 4, 4, 8
MESH = pl.DeviceIdType.MESH
F32, BF16 = jnp.float32, jnp.bfloat16

PLANE = (
    (3, 0), (0, -1), (0, 1), (1, 0), (2, 0), (0, 2), (0, -2), (1, -1),
    (3, -1), (0, 3), (0, -3), (3, 1), (1, 1), (2, -1), (0, 4), (3, 2),
    (1, 2), (3, -2), (1, -2), (2, 1), (3, 3), (1, 3), (3, -3), (1, -3),
    (2, 2), (2, -2), (3, 4), (1, 4), (2, 3), (2, -3), (2, 4),
)
ALONG_Z = (1, -1, 2, -2, 3, -3, 4)
LAG = 2


class Place:
    def __init__(self):
        pair, cd = lax.axis_index("pair"), lax.axis_index("cd")
        self.core = pair % 2
        self.z = cd // 8
        self.x = (cd // 2) % 4
        self.y = (pair // 2) * 2 + cd % 2
        self.u = self.x + self.core * (self.y - self.x)
        self.v = self.y + self.core * (self.x - self.y)

    def seat(self, core, x, y, z):
        return ((y // 2) * 2 + core, z * 8 + x * 2 + y % 2)

    def far(self, other_core):
        core = (self.core + other_core) % 2
        return self.seat(core, self.x, (self.y + 2) % 4, self.z)

    def partner(self):
        return self.seat(1 - self.core, self.x, self.y, self.z)

    def ring(self, du=0, dv=0, dz=0):
        u, v, z = (self.u + du) % 4, (self.v + dv) % 4, (self.z + dz) % 8
        return self.seat(self.core, u + self.core * (v - u), v + self.core * (u - v), z)


def split(value):
    high = value.astype(BF16)
    return high, (value - high.astype(F32)).astype(BF16)


def gather_kernel(lam_hbm, t_hbm, mu_hbm, nu_hbm, half_ref, m_ref, g_ref, w_ref,
                  lam, t_vmem, mu, nu, part, came, lam_sem, in_sem,
                  rs_send, rs_recv, u_send, u_recv, z_send, z_recv, v_send, v_recv, x_send, x_recv):
    me = Place()
    pair = lax.axis_index("pair")
    far_same = (pair + 2) % 4
    far_other = ((pair // 2 + 1) % 2) * 2 + 1 - me.core
    near = (pair // 2) * 2 + 1 - me.core
    quarters = [far_same, far_other, near, pair]

    inputs = [pltpu.make_async_copy(src, dst, in_sem.at[i])
              for i, (src, dst) in enumerate([(t_hbm, t_vmem), (mu_hbm, mu), (nu_hbm, nu)])]
    inputs[0].start()
    lam_copies = []
    for i, q in enumerate(quarters):
        cols = pl.ds(pl.multiple_of(q * 256, 256), 256)
        copy = pltpu.make_async_copy(lam_hbm.at[:, cols], lam.at[i], lam_sem.at[i])
        lam_copies.append(copy)
        if i < 2:
            copy.start()

    greeted = [me.far(0), me.far(1), me.partner(), me.ring(du=1), me.ring(du=-1), me.ring(du=2),
               *(me.ring(dz=delta) for delta in ALONG_Z), me.ring(dv=1), me.ring(dv=-1), me.ring(dv=2)]
    barrier = pltpu.get_barrier_semaphore()
    for peer in greeted:
        pl.semaphore_signal(barrier, inc=1, device_id=peer, device_id_type=MESH)

    def remote(ref, ssem, rsem, peer):
        return pltpu.make_async_remote_copy(ref, ref, ssem, rsem, device_id=peer, device_id_type=MESH)

    def arrived(ref, ssem, rsem):
        remote(ref, ssem, rsem, me.partner()).wait_recv()

    def sent(ref, ssem, rsem):
        remote(ref, ssem, rsem, me.partner()).wait_send()

    inputs[0].wait()
    t_value = t_vmem[...]
    cut = lam.shape[1] // 512 * 256
    for i in range(4):
        lam_copies[i].wait()
        if i < 2:
            lam_copies[i + 2].start()
        else:
            inputs[i - 1].start()
        part[i] = (jnp.dot(t_value[:, :cut], lam[i, :cut], preferred_element_type=F32)
                   + jnp.dot(t_value[:, cut:], lam[i, cut:], preferred_element_type=F32))
        if i == 0:
            pl.semaphore_wait(barrier, len(greeted))
        if i < 3:
            peer = (me.far(0), me.far(1), me.partner())[i]
            pltpu.make_async_remote_copy(part.at[i], came.at[i], rs_send.at[i], rs_recv.at[i],
                                         device_id=peer, device_id_type=MESH).start()

    for i in range(3):
        arrived(came.at[i], rs_send.at[i], rs_recv.at[i])
    mine = g_ref.at[me.core]
    theirs = g_ref.at[1 - me.core]
    mine[me.v, me.z, me.u] = (part[3] + came[2]) + (came[0] + came[1])

    u_of = [(me.u + d) % 4 for d in range(4)]
    v_of = [(me.v + d) % 4 for d in range(4)]
    z_of = [(me.z + d) % 8 for d in range(8)]

    def block(du, dz, dv):
        return mine.at[v_of[dv % 4], z_of[dz % 8], u_of[du % 4]]

    def z_pass(delta):
        remote(block(0, 0, 0), z_send, z_recv.at[-delta % 8 - 1], me.ring(dz=delta)).start()

    def u_pass(dz, delta):
        remote(block(0, dz, 0), u_send, u_recv.at[dz % 8, -delta % 4 - 1], me.ring(du=delta)).start()

    def v_pass(du, dz, delta):
        remote(block(du, dz, 0), v_send, v_recv.at[dz % 8], me.ring(dv=delta)).start()

    def share(dz, dv):
        unit = mine.at[v_of[dv], z_of[dz % 8]]
        remote(unit, x_send, x_recv.at[dz % 8], me.partner()).start()

    count = [0] * 8

    def have(du, dz):
        for delta in (2, 1, -1):
            v_pass(du, dz, delta)
        count[dz % 8] += 1
        if count[dz % 8] == 4:
            share(dz, 0)

    for delta in ALONG_Z:
        z_pass(delta)
    for delta in (2, 1, -1):
        u_pass(0, delta)
    have(0, 0)

    inputs[1].wait()
    inputs[2].wait()
    first = lax.axis_index("cd") * 12
    pick = (lax.broadcasted_iota(jnp.int32, (192, 768), 1)
            == first + lax.broadcasted_iota(jnp.int32, (192, 768), 0) // 16).astype(F32).astype(BF16)
    spread = (lax.broadcasted_iota(jnp.int32, (16, 256), 1) % 16
              == lax.broadcasted_iota(jnp.int32, (16, 256), 0)).astype(F32).astype(BF16)
    own_a = (lax.broadcasted_iota(jnp.int32, (192, 256), 1) // 16
             == lax.broadcasted_iota(jnp.int32, (192, 256), 0) % 16)
    for i, term in enumerate(split(nu[...])):
        taken = lax.dot_general(pick, term, (((1,), (1,)), ((), ())), preferred_element_type=F32)
        tiled = jnp.dot(taken.astype(BF16), spread, preferred_element_type=F32)
        w_ref[i] = jnp.where(own_a, tiled, 0.0).astype(BF16)
    mu_value = mu[...]
    mu_high = mu_value.astype(BF16).astype(F32)
    m_ref[...] = jnp.concatenate([mu_high, mu_high, mu_value - mu_high], axis=0).T.astype(BF16)

    for du, dz in PLANE:
        if du:
            arrived(block(du, dz, 0), u_send, u_recv.at[dz % 8, du - 1])
        else:
            arrived(block(0, dz, 0), z_send, z_recv.at[dz % 8 - 1])
            for delta in (2, 1, -1):
                u_pass(dz, delta)
        have(du, dz)

    def transform(dz):
        z = z_of[dz % 8]
        arrived(theirs.at[:, z], x_send, x_recv.at[dz % 8])
        columns = pl.ds(pl.multiple_of(z * 128, 128), 128)
        for p in range(4):
            yh, core = p // 2, p % 2
            pieces = [g_ref[core, (2 * yh + yl, x)[core], z, (x, 2 * yh + yl)[core]]
                      for x in range(NX) for yl in range(2)]
            high, low = split(jnp.concatenate(pieces, axis=0))
            both = lax.dot_general(w_ref[...].reshape(384, 256), high, nt, preferred_element_type=F32)
            value = lax.dot_general(w_ref[0], low, nt, preferred_element_type=F32) + both[:192] + both[192:]
            high, low = split(value)
            for nu_at in range(12):
                half_ref[nu_at, pl.ds(16 * p, 16), columns] = high[16 * nu_at:16 * nu_at + 16]
                half_ref[nu_at, pl.ds(16 * p + 64, 16), columns] = low[16 * nu_at:16 * nu_at + 16]

    nt = (((1,), (1,)), ((), ()))
    turns = (0,) + ALONG_Z
    for i, dz in enumerate(turns):
        arrived(mine.at[pl.ds(0, 3), z_of[dz % 8]], v_send, v_recv.at[dz % 8])
        for dv in (1, 3, 2):
            share(dz, dv)
        if i >= LAG:
            transform(turns[i - LAG])
    for dz in turns[8 - LAG:]:
        transform(dz)

    for i in range(3):
        sent(part.at[i], rs_send.at[i], rs_recv.at[i])
    sent(mine.at[0, pl.ds(0, 6)], u_send, rs_recv.at[0])
    sent(mine.at[0, pl.ds(0, 7), 0], z_send, rs_recv.at[0])
    sent(mine.at[pl.ds(0, 3)], v_send, rs_recv.at[0])
    sent(mine, x_send, rs_recv.at[0])


def transform_kernel(half_ref, m_ref, out_hbm, out, out_sem):
    def out_copy(tile, i):
        part = (pl.ds(4 * i, 4), slice(None), pl.ds(pl.multiple_of(tile * 256, 256), 256))
        return pltpu.make_async_copy(out.at[part], out_hbm.at[part], out_sem.at[tile, i])

    def step(tile, _):
        columns = pl.ds(pl.multiple_of(tile * 256, 256), 256)
        for nu in range(12):
            stacked = jnp.concatenate([half_ref[nu, :, columns], half_ref[nu, :64, columns]], axis=0)
            out[nu, :, columns] = jnp.dot(m_ref[...], stacked, preferred_element_type=F32).astype(BF16)
            if nu % 4 == 3:
                out_copy(tile, nu // 4).start()
        return 0

    lax.fori_loop(0, 4, step, 0)
    for tile in range(4):
        for i in range(3):
            out_copy(tile, i).wait()


def body(lambda_amps, t_amps, coef_mu, coef_nu):
    rows = lambda_amps.shape[0]
    hbm = pl.BlockSpec(memory_space=pltpu.HBM)
    vmem = pl.BlockSpec(memory_space=pltpu.VMEM)
    dma = pltpu.SemaphoreType.DMA
    inputs = (lambda_amps, t_amps.T, coef_mu.T, coef_nu.T)
    half, m = pl.pallas_call(
        gather_kernel,
        out_shape=(
            pltpu.VMEM((12, 128, 1024), BF16),
            pltpu.VMEM((192, 192), BF16),
        ),
        in_specs=[hbm] * 4,
        out_specs=(vmem,) * 2,
        scratch_shapes=[
            pltpu.VMEM((2, 4, NZ, 4, 16, 256), F32),
            pltpu.VMEM((2, 192, 256), BF16),
            pltpu.VMEM((4, rows, 256), BF16),
            pltpu.VMEM((16, rows), BF16),
            pltpu.VMEM((64, 192), F32),
            pltpu.VMEM((16, 768), F32),
            pltpu.VMEM((4, 16, 256), F32),
            pltpu.VMEM((3, 16, 256), F32),
            dma((4,)), dma((3,)),
            dma((3,)), dma((3,)),
            dma, dma((8, 3)),
            dma, dma((7,)),
            dma, dma((8,)),
            dma, dma((8,)),
        ],
        compiler_params=pltpu.CompilerParams(collective_id=0, has_side_effects=True, vmem_limit_bytes=20 * 2**20),
        name="gather",
    )(*(pltpu.with_memory_space_constraint(array, pltpu.HBM) for array in inputs))
    half, m = (pltpu.with_memory_space_constraint(array, pltpu.VMEM) for array in (half, m))
    out = pl.pallas_call(
        transform_kernel,
        out_shape=jax.ShapeDtypeStruct((12, 192, 1024), BF16),
        in_specs=[vmem] * 2,
        out_specs=hbm,
        scratch_shapes=[pltpu.VMEM((12, 192, 1024), BF16), dma((4, 3))],
        compiler_params=pltpu.CompilerParams(vmem_limit_bytes=32 * 2**20),
        name="transform",
    )(half, m)
    return jnp.transpose(out, (1, 0, 2))


def solution(mesh):
    in_specs = (P("pair", None), P("pair", "cd"), P("pair", None), P())
    out_specs = P("pair", "cd", None)
    return jax.shard_map(body, mesh=mesh, in_specs=in_specs, out_specs=out_specs, check_vma=False)
```

time: 140 us -> 38 us (0.27)
  blocking collectives: 42.6 us -> 0 us
  Pallas kernels: 0 us -> 37.9 us
  waiting for transfers between devices: 33.2 us -> 0 us
  local copies, waits for them, and re-layouts: 31.5 us -> 0 us
  matrix products: 15.8 us -> 0 us
  between operations: 13.4 us -> 0.01 us
  other arithmetic: 2.61 us -> 0 us
    all_to_all x2 -> x0, blocking collectives: 42.6 us -> none  [the longest x1 32.1 us: body(): moved = lax.all_to_all(half, 'cd', split_axis=0, concat_axis=2, tiled=True)]
    pallas_call x0 -> x2, Pallas kernels: none -> 37.9 us  [the longest x1 35.1 us: body(): pl.pallas_call(gather_kernel, out_shape=(pltpu.VMEM((12, 128, 1024), BF16...]
    all_gather x1 -> x0, waiting for transfers between devices: 33.2 us -> none  [body(): gathered = lax.all_gather(moved, 'pair', axis=1, tiled=True)]
    all_to_all x3 -> x0, local copies, waits for them, and re-layouts: 16.7 us -> none  [body(): moved = lax.all_to_all(half, 'cd', split_axis=0, concat_axis=2, tiled=True)]
    dot_general x3 -> x0, matrix products: 15.8 us -> none  [the longest x1 10.6 us: body(): jnp.einsum('ma,nac->mnc', coef_mu, gathered, precision=lax.Precision.HIGH...]
    unnamed x8 -> x0, local copies, waits for them, and re-layouts: 9.51 us -> none
    dot_general x1 -> x0, local copies, waits for them, and re-layouts: 4.98 us -> none  [body(): jnp.einsum('abc,nb->nac', panel, coef_nu, precision=lax.Precision.HIGHEST)]
    all_to_all x1 -> x0, other arithmetic: 2.6 us -> none  [body(): moved = lax.all_to_all(half, 'cd', split_axis=0, concat_axis=2, tiled=True)]
  transfers between devices with their start and end apart: 1 -> 0, of which waited for: 1 -> 0; matrix products, arithmetic and copies ran while one was open for 0% -> 0% of each run, Pallas kernels for 0% -> 0%
where the time goes in v2:
time: 38 us; the launch traced here: 37.9 us
  Pallas kernels  37.9 us (100%)
    pallas_call x1, Pallas kernels, body(): pl.pallas_call(gather_kernel, out_shape=(pltpu.VMEM((12, 128, 1024), BF16...  35.1 us
    pallas_call x1, Pallas kernels, body(): pl.pallas_call(transform_kernel, out_shape=jax.ShapeDtypeStruct((12, 192,...  2.79 us

profile of v2, /device:TPU:1, one launch (start us, length us, event | category | flops | bytes accessed | tf_op | source)
XLA Modules:
  0.0 37.9 jit_solution(1086663175135576411)
XLA Ops:
  0.0 35.1 %gather.1 = (bf16[12,128,1024]{2,1,0:T(8,128)(2,1)S(1)}, bf16[192,192]{1,0:T(8,128)(2,1)S(1)}) custom-call(bf16[2816,1024]{1,0:T(8,128)(2,1)} %lam_hbm.1, bf16[16,2816]{1,0:T(8,128)(2,1)} %bitcast.4, f32[64,192]{1,0:T(8,128)} %bitcast.5, f32[16,768]{1,0:T(8,128)} %bitcast.6), custom_call_target="tpu_custom_call" | custom-call | tf_op jit(solution)/shard_map/gather/pallas_call | solution.py:236
  35.1 2.8 %transform.1 = bf16[12,192,1024]{2,1,0:T(8,128)(2,1)} custom-call(bf16[12,128,1024]{2,1,0:T(8,128)(2,1)S(1)} %get-tuple-element.7.half_ref, bf16[192,192]{1,0:T(8,128)(2,1)S(1)} %get-tuple-element.8.m_ref), custom_call_target="tpu_custom_call" | custom-call | tf_op jit(solution)/shard_map/transform/pallas_call | solution.py:264

commit v3 on v2

--- a/solution.py
+++ b/solution.py
@@ -12,12 +12,14 @@
 F32, BF16 = jnp.float32, jnp.bfloat16
 
 PLANE = (
-    (3, 0), (0, -1), (0, 1), (1, 0), (2, 0), (0, 2), (0, -2), (1, -1),
-    (3, -1), (0, 3), (0, -3), (3, 1), (1, 1), (2, -1), (0, 4), (3, 2),
-    (1, 2), (3, -2), (1, -2), (2, 1), (3, 3), (1, 3), (3, -3), (1, -3),
-    (2, 2), (2, -2), (3, 4), (1, 4), (2, 3), (2, -3), (2, 4),
+    (0, 1), (0, -1), (1, 0), (3, 0), (0, 2), (0, -2), (2, 0), (0, 3),
+    (0, -3), (0, 4), (1, 1), (1, -1), (1, 2), (1, -2), (3, 1), (3, -1),
+    (3, 2), (3, -2), (2, 1), (2, -1), (2, 2), (2, -2), (1, 3), (3, 3),
+    (2, 3), (1, -3), (3, -3), (2, -3), (1, 4), (3, 4), (2, 4),
 )
+
 ALONG_Z = (1, -1, 2, -2, 3, -3, 4)
+NEAR_Z = (2, -2, 1, -1)
 LAG = 2
 
 
@@ -118,8 +120,8 @@
     def block(du, dz, dv):
         return mine.at[v_of[dv % 4], z_of[dz % 8], u_of[du % 4]]
 
-    def z_pass(delta):
-        remote(block(0, 0, 0), z_send, z_recv.at[-delta % 8 - 1], me.ring(dz=delta)).start()
+    def z_pass(du, delta):
+        remote(block(du, 0, 0), z_send.at[min(du, 1)], z_recv.at[du, -delta % 8 - 1], me.ring(dz=delta)).start()
 
     def u_pass(dz, delta):
         remote(block(0, dz, 0), u_send, u_recv.at[dz % 8, -delta % 4 - 1], me.ring(du=delta)).start()
@@ -141,7 +143,7 @@
             share(dz, 0)
 
     for delta in ALONG_Z:
-        z_pass(delta)
+        z_pass(0, delta)
     for delta in (2, 1, -1):
         u_pass(0, delta)
     have(0, 0)
@@ -164,10 +166,14 @@
     m_ref[...] = jnp.concatenate([mu_high, mu_high, mu_value - mu_high], axis=0).T.astype(BF16)
 
     for du, dz in PLANE:
-        if du:
+        if dz == 0 or (du and dz not in NEAR_Z):
             arrived(block(du, dz, 0), u_send, u_recv.at[dz % 8, du - 1])
         else:
-            arrived(block(0, dz, 0), z_send, z_recv.at[dz % 8 - 1])
+            arrived(block(du, dz, 0), z_send.at[0], z_recv.at[du, dz % 8 - 1])
+        if dz == 0:
+            for delta in NEAR_Z:
+                z_pass(du, delta)
+        elif du == 0 and dz not in NEAR_Z:
             for delta in (2, 1, -1):
                 u_pass(dz, delta)
         have(du, dz)
@@ -201,8 +207,9 @@
 
     for i in range(3):
         sent(part.at[i], rs_send.at[i], rs_recv.at[i])
-    sent(mine.at[0, pl.ds(0, 6)], u_send, rs_recv.at[0])
-    sent(mine.at[0, pl.ds(0, 7), 0], z_send, rs_recv.at[0])
+    sent(mine.at[0, pl.ds(0, 8 - len(NEAR_Z)), pl.ds(0, 3)], u_send, rs_recv.at[0])
+    sent(mine.at[0, pl.ds(0, 7), 0], z_send.at[0], rs_recv.at[0])
+    sent(mine.at[0, pl.ds(0, len(NEAR_Z)), pl.ds(0, 3)], z_send.at[1], rs_recv.at[0])
     sent(mine.at[pl.ds(0, 3)], v_send, rs_recv.at[0])
     sent(mine, x_send, rs_recv.at[0])
 
@@ -253,7 +260,7 @@
             dma((4,)), dma((3,)),
             dma((3,)), dma((3,)),
             dma, dma((8, 3)),
-            dma, dma((7,)),
+            dma((2,)), dma((4, 7)),
             dma, dma((8,)),
             dma, dma((8,)),
         ],

time: 38 us -> 36.3 us (0.955)
  Pallas kernels: 37.9 us -> 36.1 us
    pallas_call x1, Pallas kernels: 35.1 us -> 33.3 us  [body(): pl.pallas_call(gather_kernel, out_shape=(pltpu.VMEM((12, 128, 1024), BF16...]
where the time goes in v3:
time: 36.3 us; the launch traced here: 36.1 us
  Pallas kernels  36.1 us (99%)
    pallas_call x1, Pallas kernels, body(): pl.pallas_call(gather_kernel, out_shape=(pltpu.VMEM((12, 128, 1024), BF16...  33.3 us
    pallas_call x1, Pallas kernels, body(): pl.pallas_call(transform_kernel, out_shape=jax.ShapeDtypeStruct((12, 192,...  2.79 us

profile of v3, /device:TPU:1, one launch (start us, length us, event | category | flops | bytes accessed | tf_op | source)
XLA Modules:
  0.0 36.1 jit_solution(18437250043943564225)
XLA Ops:
  0.0 33.3 %gather.1 = (bf16[12,128,1024]{2,1,0:T(8,128)(2,1)S(1)}, bf16[192,192]{1,0:T(8,128)(2,1)S(1)}) custom-call(bf16[2816,1024]{1,0:T(8,128)(2,1)} %lam_hbm.1, bf16[16,2816]{1,0:T(8,128)(2,1)} %bitcast.4, f32[64,192]{1,0:T(8,128)} %bitcast.5, f32[16,768]{1,0:T(8,128)} %bitcast.6), custom_call_target="tpu_custom_call" | custom-call | tf_op jit(solution)/shard_map/gather/pallas_call | solution.py:243
  33.4 2.8 %transform.1 = bf16[12,192,1024]{2,1,0:T(8,128)(2,1)} custom-call(bf16[12,128,1024]{2,1,0:T(8,128)(2,1)S(1)} %get-tuple-element.7.half_ref, bf16[192,192]{1,0:T(8,128)(2,1)S(1)} %get-tuple-element.8.m_ref), custom_call_target="tpu_custom_call" | custom-call | tf_op jit(solution)/shard_map/transform/pallas_call | solution.py:271

commit v4 on v3

--- a/solution.py
+++ b/solution.py
@@ -19,7 +19,7 @@
 )
 
 ALONG_Z = (1, -1, 2, -2, 3, -3, 4)
-NEAR_Z = (2, -2, 1, -1)
+NEAR_Z = (1, -1, 2, -2)
 LAG = 2
 
 
@@ -216,7 +216,7 @@
 
 def transform_kernel(half_ref, m_ref, out_hbm, out, out_sem):
     def out_copy(tile, i):
-        part = (pl.ds(4 * i, 4), slice(None), pl.ds(pl.multiple_of(tile * 256, 256), 256))
+        part = (pl.ds(2 * i, 2), slice(None), pl.ds(pl.multiple_of(tile * 256, 256), 256))
         return pltpu.make_async_copy(out.at[part], out_hbm.at[part], out_sem.at[tile, i])
 
     def step(tile, _):
@@ -224,13 +224,13 @@
         for nu in range(12):
             stacked = jnp.concatenate([half_ref[nu, :, columns], half_ref[nu, :64, columns]], axis=0)
             out[nu, :, columns] = jnp.dot(m_ref[...], stacked, preferred_element_type=F32).astype(BF16)
-            if nu % 4 == 3:
-                out_copy(tile, nu // 4).start()
+            if nu % 2 == 1:
+                out_copy(tile, nu // 2).start()
         return 0
 
     lax.fori_loop(0, 4, step, 0)
     for tile in range(4):
-        for i in range(3):
+        for i in range(6):
             out_copy(tile, i).wait()
 
 
@@ -273,7 +273,7 @@
         out_shape=jax.ShapeDtypeStruct((12, 192, 1024), BF16),
         in_specs=[vmem] * 2,
         out_specs=hbm,
-        scratch_shapes=[pltpu.VMEM((12, 192, 1024), BF16), dma((4, 3))],
+        scratch_shapes=[pltpu.VMEM((12, 192, 1024), BF16), dma((4, 6))],
         compiler_params=pltpu.CompilerParams(vmem_limit_bytes=32 * 2**20),
         name="transform",
     )(half, m)

time: 36.3 us -> 36.4 us (level)
  no operation moved by 1% of the time
where the time goes in v4:
time: 36.4 us; the launch traced here: 36.2 us
  Pallas kernels  36.2 us (99%)
    pallas_call x1, Pallas kernels, body(): pl.pallas_call(gather_kernel, out_shape=(pltpu.VMEM((12, 128, 1024), BF16...  33.3 us
    pallas_call x1, Pallas kernels, body(): pl.pallas_call(transform_kernel, out_shape=jax.ShapeDtypeStruct((12, 192,...  2.83 us

profile of v4, /device:TPU:1, one launch (start us, length us, event | category | flops | bytes accessed | tf_op | source)
XLA Modules:
  0.0 36.2 jit_solution(7926942531339709411)
XLA Ops:
  0.0 33.3 %gather.1 = (bf16[12,128,1024]{2,1,0:T(8,128)(2,1)S(1)}, bf16[192,192]{1,0:T(8,128)(2,1)S(1)}) custom-call(bf16[2816,1024]{1,0:T(8,128)(2,1)} %lam_hbm.1, bf16[16,2816]{1,0:T(8,128)(2,1)} %bitcast.4, f32[64,192]{1,0:T(8,128)} %bitcast.5, f32[16,768]{1,0:T(8,128)} %bitcast.6), custom_call_target="tpu_custom_call" | custom-call | tf_op jit(solution)/shard_map/gather/pallas_call | solution.py:243
  33.4 2.8 %transform.1 = bf16[12,192,1024]{2,1,0:T(8,128)(2,1)} custom-call(bf16[12,128,1024]{2,1,0:T(8,128)(2,1)S(1)} %get-tuple-element.7.half_ref, bf16[192,192]{1,0:T(8,128)(2,1)S(1)} %get-tuple-element.8.m_ref), custom_call_target="tpu_custom_call" | custom-call | tf_op jit(solution)/shard_map/transform/pallas_call | solution.py:271
